TPU v7x, 512 devices: a whole 4x8x8 slice. The times are simulated.
512 devices in a mesh: occ: 16 (over x, z_lo), sec: 32 (over z_hi, y, core).
Axes of the slice: x: 4, y: 8, z: 8 (z_hi: 2, z_lo: 4; z = z_hi * 4 + z_lo), core: 2. Of those that a mesh axis runs over, the one named last changes fastest.
Arguments:
- amplitudes: float32 [768, 512, 512], P('occ', None, 'sec'), may hold values from -5 to 5
- live_pairs: int32 [16], replicated, may hold values from 12 to 48, as said below
- ladder_ints: float32 [512, 512, 1024], P('occ', 'sec'), may hold values from -0.0234375 to 0.0234375
- cycle_ints: float32 [48, 512, 6144], P(None, 'sec', 'occ'), may hold values from -0.0390625 to 0.0390625
- pair_ints: float32 [768, 1024], P('occ', 'sec'), may hold values from -6 to 6
- occ_energy: float32 [48], replicated, may hold values from -2 to -0.5
- vir_energy: float32 [512], replicated, may hold values from 0.5 to 4
Outputs:
- new_amplitudes: float32 [768, 1024], P('occ', 'sec')
Inputs may be any that keep to these rules, and one draw needn't show every extreme that they name: live_pairs[o] live pairs are the first ones of owner o's 48 pairs; some owner has all of its pairs live.
All inputs are finite; a program needn't handle non-finite values.
Results may differ from a plain program's by a relative error of at most 0.00005.
Values sent between devices are 32-bit elements; how exact they have to be, the bound alone decides.
A program may use at most 64 MiB of HBM per device.

v0:
```python
import jax
import jax.numpy as jnp
from jax import lax
from jax.sharding import PartitionSpec as P

OCCUPIED = 48
VIRTUAL = 512
A_WINDOW = 8
B_WINDOW = 128
I_OWNER = 1


highest = lax.Precision.HIGHEST


def copy_for_each(array, axis):
    devices = lax.axis_size(axis)
    return lax.all_to_all(
        jnp.broadcast_to(array[None], (devices, *array.shape)), axis, 0, 0, tiled=True
    )


def laid_out(tiles, dim):
    tiles = jnp.moveaxis(tiles, 0, dim)
    lengths = tiles.shape
    return tiles.reshape(*lengths[:dim], lengths[dim] * lengths[dim + 1], *lengths[dim + 2 :])


def gather_directly(array, axis, dim):
    tiles = copy_for_each(array, axis)
    return laid_out(tiles, dim)


def split_up(array, dim, devices):
    lengths = array.shape
    tiles = array.reshape(*lengths[:dim], devices, lengths[dim] // devices, *lengths[dim + 1 :])
    return jnp.moveaxis(tiles, dim, 0)


def sent_and_summed(array, axis, dim):
    devices = lax.axis_size(axis)
    tiles = lax.all_to_all(split_up(array, dim, devices), axis, 0, 0, tiled=True)
    return jnp.sum(tiles, axis=0)


def shards(amplitudes, live_pairs, ladder_ints, cycle_ints, pair_ints, occ_energy, vir_energy):
    owners = lax.axis_size("occ")
    sections = lax.axis_size("sec")
    owner_index = lax.axis_index("occ")
    section = lax.axis_index("sec")
    owner_rows = I_OWNER * OCCUPIED
    window_rows = I_OWNER * owners
    owner_cols = OCCUPIED // owners
    col_share = A_WINDOW * B_WINDOW // sections
    d_share = amplitudes.shape[2]
    live_count = lax.dynamic_slice_in_dim(live_pairs, owner_index, 1)[0]
    local_rows = lax.broadcasted_iota(jnp.int32, (owner_rows, 1, 1), 0)
    live_rows = (local_rows < live_count).astype(jnp.float32)
    masked = amplitudes * live_rows
    flat_tiles = masked.reshape(owner_rows, owners, VIRTUAL // owners * d_share)
    regrouped = lax.all_to_all(flat_tiles, "occ", split_axis=1, concat_axis=0, tiled=True)
    pair_total = regrouped.shape[0]
    ladder_part = 0.5 * jnp.dot(
        regrouped.reshape(pair_total, -1),
        ladder_ints.reshape(-1, A_WINDOW * B_WINDOW),
        precision=highest,
        preferred_element_type=jnp.float32,
    )
    cycle_local = masked[:, :A_WINDOW, :].reshape(owner_rows, A_WINDOW * d_share)
    cycle_flat = gather_directly(cycle_local, "occ", 0)
    cycle_rows = cycle_flat.reshape(window_rows, OCCUPIED, A_WINDOW, d_share)
    cycle_part = jnp.einsum(
        "ikac,kcn->ian",
        cycle_rows,
        cycle_ints,
        precision=highest,
        preferred_element_type=jnp.float32,
    )
    cycle_part = (
        cycle_part.reshape(window_rows, A_WINDOW, owner_cols, B_WINDOW)
        .transpose(0, 2, 1, 3)
        .reshape(window_rows, owner_cols, A_WINDOW * B_WINDOW)
    )
    ladder_grid = ladder_part.reshape(window_rows, OCCUPIED, A_WINDOW * B_WINDOW)
    offset = owner_index * owner_cols
    current_part = lax.dynamic_slice_in_dim(ladder_grid, offset, owner_cols, 1)
    ladder_grid = lax.dynamic_update_slice_in_dim(ladder_grid, current_part + cycle_part, offset, 1)
    combined = ladder_grid.reshape(pair_total, A_WINDOW * B_WINDOW)
    first_sum = sent_and_summed(combined, "occ", 0)
    summed = sent_and_summed(first_sum, "sec", 1)
    residual = summed + pair_ints
    occ_rows = lax.dynamic_slice_in_dim(occ_energy, owner_index * I_OWNER, I_OWNER)
    pair_energy = (occ_rows[:, None] + occ_energy[None, :]).reshape(owner_rows, 1)
    vir_pairs = (vir_energy[:A_WINDOW, None] + vir_energy[None, :B_WINDOW]).reshape(
        A_WINDOW * B_WINDOW
    )
    vir_cols = lax.dynamic_slice_in_dim(vir_pairs, section * col_share, col_share)
    denominator = pair_energy - vir_cols[None, :]
    live_out = (lax.broadcasted_iota(jnp.int32, (owner_rows, 1), 0) < live_count).astype(
        jnp.float32
    )
    return residual / denominator * live_out


def solution(mesh):
    in_specs = (
        P("occ", None, "sec"),
        P(),
        P("occ", "sec", None),
        P(None, "sec", "occ"),
        P("occ", "sec"),
        P(),
        P(),
    )
    out_specs = P("occ", "sec")
    return jax.shard_map(shards, mesh=mesh, in_specs=in_specs, out_specs=out_specs, check_vma=False)
```

profile of v0, /device:TPU:1, one launch (start us, length us, event | category | flops | bytes accessed | tf_op | source)
XLA Modules:
  0.0 196.8 jit_solution(14214271201332884352)
XLA Ops:
  0.0 0.0 copy-start
  0.0 1.4 dynamic_slice.12
  1.4 0.6 compare_convert_fusion
  2.0 1.6 broadcast_multiply_fusion
  3.6 0.0 copy-start.2
  3.6 1.2 copy-done.2
  4.8 0.1 slice.12
  4.9 0.2 copy.36
  5.1 0.1 copy.37
  5.1 0.8 broadcast_in_dim.5
  5.9 10.4 %all-to-all-start.1 = ((f32[16,48,128]{2,1,0:T(8,128)}), f32[16,48,128]{2,1,0:T(8,128)S(1)}, u32[]{:S(2)}, u32[]{:S(2)}) async-start(f32[16,48,128]{2,1,0:T(8,128)} %broadcast_in_dim.5), calls=%async_computation.1 | async-start | bytes 786432 | tf_op jit(solution)/shard_map/all_to_all | solution.py:18
  16.3 5.0 %copy.33 = f32[48,512,16]{0,2,1:T(8,128)} copy(f32[48,512,16]{1,2,0:T(8,128)} %copy-done.2) | data formatting | bytes 3145728 | tf_op jit(solution)/shard_map/mul | solution.py:59
  21.3 3.7 %copy.34 = f32[48,16,512]{2,0,1:T(8,128)} copy(f32[48,16,512]{0,2,1:T(8,128)} %bitcast.40) | data formatting | bytes 3145728 | tf_op jit(solution)/shard_map/reshape | solution.py:60
  25.0 4.2 %all-to-all-done.1 = f32[16,48,128]{2,1,0:T(8,128)S(1)} async-done(((f32[16,48,128]{2,1,0:T(8,128)}), f32[16,48,128]{2,1,0:T(8,128)S(1)}, u32[]{:S(2)}, u32[]{:S(2)}) %all-to-all-start.1) | async-done | bytes 393248 | tf_op jit(solution)/shard_map/all_to_all | solution.py:18
  29.2 4.4 %all-to-all-start = ((f32[48,16,512]{2,0,1:T(8,128)}), f32[48,16,512]{2,0,1:T(8,128)}, u32[]{:S(2)}, u32[]{:S(2)}) async-start(f32[48,16,512]{2,0,1:T(8,128)} %copy.34), calls=%async_computation | async-start | bytes 3145728 | tf_op jit(solution)/shard_map/all_to_all | solution.py:61
  33.6 2.8 %reshape.59 = f32[3,128,16,48]{1,0,2,3:T(4,128)} reshape(f32[384,16,48]{0,1,2:T(8,128)} %bitcast.46) | data formatting | bytes 2359296 | tf_op jit(solution)/shard_map/ikac,kcn->ian/dot_general | solution.py:72
  36.4 0.3 copy.38
  36.8 3.5 %fusion.3 = f32[16,3,8,128]{3,2,1,0:T(8,128)S(1)} fusion(f32[3,128,16,48]{1,0,2,3:T(4,128)} %reshape.59, f32[16,48,8,16,1]{1,3,2,0,4:T(8,128)S(1)} %bitcast.43), kind=kOutput, calls=%fused_computation.4 | convolution fusion | flops 452984832 | bytes 1769472 | tf_op jit(solution)/shard_map/ikac,kcn->ian/dot_general | solution.py:72
  40.4 31.5 %all-to-all-done = f32[48,16,512]{2,0,1:T(8,128)} async-done(((f32[48,16,512]{2,0,1:T(8,128)}), f32[48,16,512]{2,0,1:T(8,128)}, u32[]{:S(2)}, u32[]{:S(2)}) %all-to-all-start) | async-done | bytes 1572896 | tf_op jit(solution)/shard_map/all_to_all | solution.py:61
  71.9 0.0 copy-done
  71.9 6.8 %convolution_multiply_fusion = f32[768,1024]{1,0:T(8,128)S(1)} fusion(f32[768,512]{1,0:T(8,128)} %bitcast.4, f32[512,1024]{1,0:T(8,128)S(1)} %bitcast.39), kind=kOutput, calls=%fused_computation | convolution fusion | flops 4832624640 | bytes 6815744 | tf_op jit(solution)/shard_map/dot_general | solution.py:63
  78.7 0.0 copy-start.1
  78.7 1.7 copy-done.1
  80.4 0.1 constant_dynamic-slice_fusion
  80.5 0.1 copy_add_fusion
  80.6 0.1 copy.43
  80.7 3.7 %dynamic_update_slice.3 = f32[16,48,1024]{2,1,0:T(8,128)} dynamic-update-slice(f32[16,48,1024]{2,1,0:T(8,128)} %bitcast.42, f32[16,3,1024]{2,1,0:T(4,128)S(1)} %copy.43, s32[]{:T(128)} %constant.5.clone.1, s32[]{:T(128)S(6)} %select_n.14, s32[]{:T(128)} %constant.5.clone.1) | dynamic-update-slice | bytes 393220 | tf_op jit(solution)/shard_map/dynamic_update_slice | solution.py:87
  84.4 4.9 %all-to-all-start.2 = ((f32[16,48,1024]{2,1,0:T(8,128)}), f32[16,48,1024]{2,1,0:T(8,128)}, u32[]{:S(2)}, u32[]{:S(2)}) async-start(f32[16,48,1024]{2,1,0:T(8,128)} %dynamic_update_slice.3), calls=%async_computation.2 | async-start | bytes 6291456 | tf_op jit(solution)/shard_map/all_to_all | solution.py:42
  89.3 0.0 copy-done.4
  89.3 0.6 dynamic_slice.14
  89.9 71.7 %all-to-all-done.2 = f32[16,48,1024]{2,1,0:T(8,128)} async-done(((f32[16,48,1024]{2,1,0:T(8,128)}), f32[16,48,1024]{2,1,0:T(8,128)}, u32[]{:S(2)}, u32[]{:S(2)}) %all-to-all-start.2) | async-done | bytes 3145760 | tf_op jit(solution)/shard_map/all_to_all | solution.py:42
  161.6 2.1 %reduce_sum.18 = f32[48,1024]{1,0:T(8,128)S(1)} reduce(f32[16,48,1024]{2,1,0:T(8,128)} %all-to-all-done.2, f32[]{:T(128)} %constant.10.clone.1), dimensions={0}, to_apply=%region_0.0 | reduce | flops 737280 | bytes 3342340 | tf_op jit(solution)/shard_map/reduce_sum | solution.py:43
  163.7 0.0 slice-start
  163.7 0.0 slice-start.1
  163.7 0.2 reshape.55
  163.9 0.5 copy.44
  164.4 1.2 reshape.60
  165.6 14.5 %all-to-all-start.3 = ((f32[32,1,1536]{2,1,0:T(1,128)}), f32[32,1,1536]{2,1,0:T(1,128)S(1)}, u32[]{:S(2)}, u32[]{:S(2)}) async-start(f32[32,1,1536]{2,1,0:T(1,128)} %reshape.60), calls=%async_computation.3 | async-start | bytes 393216 | tf_op jit(solution)/shard_map/all_to_all | solution.py:42
  180.1 0.0 slice-done
  180.1 0.1 add_bitcast_fusion
  180.1 0.1 dynamic_slice.15
  180.2 0.6 broadcast_add_fusion
  180.9 13.3 %all-to-all-done.3 = f32[32,1,1536]{2,1,0:T(1,128)S(1)} async-done(((f32[32,1,1536]{2,1,0:T(1,128)}), f32[32,1,1536]{2,1,0:T(1,128)S(1)}, u32[]{:S(2)}, u32[]{:S(2)}) %all-to-all-start.3) | async-done | bytes 196640 | tf_op jit(solution)/shard_map/all_to_all | solution.py:42
  194.2 0.5 broadcast.18
  194.7 1.1 reduce
  195.8 0.2 reshape.61
  196.0 0.1 bitcast_reduce_fusion
  196.1 0.7 divide_multiply_fusion
  (6 shorter events, 0.1 us)
Async XLA Ops:
  0.0 71.9 %copy-start = (f32[32,16,1024]{2,1,0:T(8,128)S(1)}, f32[32,16,1024]{2,1,0:T(8,128)}, u32[]{:S(2)}) copy-start(f32[32,16,1024]{2,1,0:T(8,128)} %param.9) | copy-start | bytes 6291460
  3.6 1.2 copy-start.2
  5.9 23.3 %all-to-all-start.1 = ((f32[16,48,128]{2,1,0:T(8,128)}), f32[16,48,128]{2,1,0:T(8,128)S(1)}, u32[]{:S(2)}, u32[]{:S(2)}) async-start(f32[16,48,128]{2,1,0:T(8,128)} %broadcast_in_dim.5), calls=%async_computation.1 | async-start | bytes 786432 | tf_op jit(solution)/shard_map/all_to_all | solution.py:18
  29.2 42.6 %all-to-all-start = ((f32[48,16,512]{2,0,1:T(8,128)}), f32[48,16,512]{2,0,1:T(8,128)}, u32[]{:S(2)}, u32[]{:S(2)}) async-start(f32[48,16,512]{2,0,1:T(8,128)} %copy.34), calls=%async_computation | async-start | bytes 3145728 | tf_op jit(solution)/shard_map/all_to_all | solution.py:61
  78.7 1.7 copy-start.1
  84.4 4.9 %copy-start.4 = (f32[48]{0:T(128)S(1)}, f32[48]{0:T(128)}, u32[]{:S(2)}) copy-start(f32[48]{0:T(128)} %param.12) | copy-start | bytes 580
  84.4 77.2 %all-to-all-start.2 = ((f32[16,48,1024]{2,1,0:T(8,128)}), f32[16,48,1024]{2,1,0:T(8,128)}, u32[]{:S(2)}, u32[]{:S(2)}) async-start(f32[16,48,1024]{2,1,0:T(8,128)} %dynamic_update_slice.3), calls=%async_computation.2 | async-start | bytes 6291456 | tf_op jit(solution)/shard_map/all_to_all | solution.py:42
  163.7 16.4 %slice-start = ((f32[512]{0:T(512)}), f32[128]{0:T(128)S(1)}, s32[]{:S(2)}) async-start(f32[512]{0:T(512)} %param.13), calls=%async_computation.4 | async-start | bytes 1024 | tf_op jit(solution)/shard_map/slice | solution.py:94
  163.7 16.4 %slice-start.1 = ((f32[512]{0:T(512)}), f32[8]{0:T(128)S(1)}, s32[]{:S(2)}) async-start(f32[512]{0:T(512)} %param.13), calls=%async_computation.5 | async-start | bytes 1024 | tf_op jit(solution)/shard_map/slice | solution.py:94
  164.4 31.7 %copy-start.3 = (f32[48,32]{0,1:T(8,128)S(1)}, f32[48,32]{0,1:T(8,128)}, u32[]{:S(2)}) copy-start(f32[48,32]{0,1:T(8,128)} %param.11) | copy-start | bytes 18436
  165.6 28.6 %all-to-all-start.3 = ((f32[32,1,1536]{2,1,0:T(1,128)}), f32[32,1,1536]{2,1,0:T(1,128)S(1)}, u32[]{:S(2)}, u32[]{:S(2)}) async-start(f32[32,1,1536]{2,1,0:T(1,128)} %reshape.60), calls=%async_computation.3 | async-start | bytes 393216 | tf_op jit(solution)/shard_map/all_to_all | solution.py:42
where the time goes:
time: 197 us
  waiting for transfers between devices  121 us (61%)
  starting transfers between devices  34.1 us (17%)
  local copies, waits for them, and re-layouts  24.4 us (12%)
  matrix products  10.3 us (5%)
  other arithmetic  7 us (4%)
    all_to_all x2, waiting for transfers between devices, sent_and_summed(): lax.all_to_all(split_up(array, dim, devices), axis, 0, 0, tiled=True)  85 us
    all_to_all x1, waiting for transfers between devices, shards(): lax.all_to_all(flat_tiles, 'occ', split_axis=1, concat_axis=0, tiled=True)  31.5 us
    all_to_all x2, starting transfers between devices, sent_and_summed(): lax.all_to_all(split_up(array, dim, devices), axis, 0, 0, tiled=True)  19.3 us
    all_to_all x1, starting transfers between devices, copy_for_each(): lax.all_to_all(jnp.broadcast_to(array[None], (devices, *array.shape)), ax...  10.4 us
    dot_general x1, matrix products, shards(): jnp.dot(regrouped.reshape(pair_total, -1), ladder_ints.reshape(-1, A_WIND...  6.81 us
    mul x1, local copies, waits for them, and re-layouts, shards(): masked = amplitudes * live_rows  5 us
    all_to_all x1, starting transfers between devices, shards(): lax.all_to_all(flat_tiles, 'occ', split_axis=1, concat_axis=0, tiled=True)  4.4 us
    unnamed x12, local copies, waits for them, and re-layouts  4.26 us
  transfers between devices with their start and end apart: 4, of which 4 were waited for; matrix products, arithmetic and copies ran while one was open for 9% of the time, Pallas kernels for 0%

commit v1 on v0

--- a/solution.py
+++ b/solution.py
@@ -10,7 +10,7 @@
 I_OWNER = 1
 
 
-highest = lax.Precision.HIGHEST
+highest = lax.Precision.HIGH
 
 
 def copy_for_each(array, axis):
@@ -29,18 +29,6 @@
 def gather_directly(array, axis, dim):
     tiles = copy_for_each(array, axis)
     return laid_out(tiles, dim)
-
-
-def split_up(array, dim, devices):
-    lengths = array.shape
-    tiles = array.reshape(*lengths[:dim], devices, lengths[dim] // devices, *lengths[dim + 1 :])
-    return jnp.moveaxis(tiles, dim, 0)
-
-
-def sent_and_summed(array, axis, dim):
-    devices = lax.axis_size(axis)
-    tiles = lax.all_to_all(split_up(array, dim, devices), axis, 0, 0, tiled=True)
-    return jnp.sum(tiles, axis=0)
 
 
 def shards(amplitudes, live_pairs, ladder_ints, cycle_ints, pair_ints, occ_energy, vir_energy):
@@ -86,8 +74,8 @@
     current_part = lax.dynamic_slice_in_dim(ladder_grid, offset, owner_cols, 1)
     ladder_grid = lax.dynamic_update_slice_in_dim(ladder_grid, current_part + cycle_part, offset, 1)
     combined = ladder_grid.reshape(pair_total, A_WINDOW * B_WINDOW)
-    first_sum = sent_and_summed(combined, "occ", 0)
-    summed = sent_and_summed(first_sum, "sec", 1)
+    first_sum = lax.psum_scatter(combined, "sec", scatter_dimension=1, tiled=True)
+    summed = lax.psum_scatter(first_sum, "occ", scatter_dimension=0, tiled=True)
     residual = summed + pair_ints
     occ_rows = lax.dynamic_slice_in_dim(occ_energy, owner_index * I_OWNER, I_OWNER)
     pair_energy = (occ_rows[:, None] + occ_energy[None, :]).reshape(owner_rows, 1)

time: 197 us -> 329 us (1.67)
  the two profiles are of different devices: /device:TPU:1 before, /device:TPU:8 now
where the time goes in v1:
time: 329 us
  waiting for transfers between devices  262 us (80%)
  local copies, waits for them, and re-layouts  28.4 us (9%)
  starting transfers between devices  14.3 us (4%)
  between operations  13.5 us (4%)
  matrix products  7.1 us (2%)
  other arithmetic  3.76 us (1%)
    unnamed x4, waiting for transfers between devices  225 us
    all_to_all x1, waiting for transfers between devices, shards(): lax.all_to_all(flat_tiles, 'occ', split_axis=1, concat_axis=0, tiled=True)  32 us
    all_to_all x1, starting transfers between devices, copy_for_each(): lax.all_to_all(jnp.broadcast_to(array[None], (devices, *array.shape)), ax...  9.83 us
    unnamed x13, local copies, waits for them, and re-layouts  9.53 us
  transfers between devices with their start and end apart: 4, of which 4 were waited for; matrix products, arithmetic and copies ran while one was open for 5% of the time, Pallas kernels for 0%

profile of v1, /device:TPU:8, one launch (start us, length us, event | category | flops | bytes accessed | tf_op | source)
XLA Modules:
  0.0 328.7 jit_solution(5443980541460384650)
XLA Ops:
  6.5 0.0 copy-start
  6.5 1.4 dynamic_slice.12
  7.9 0.6 compare_convert_fusion
  8.6 1.6 broadcast_multiply_fusion
  10.2 0.0 copy-start.2
  10.2 1.2 copy-done.2
  11.3 0.1 slice.12
  11.4 0.2 copy.49
  11.6 0.1 copy.50
  11.7 0.8 broadcast_in_dim.5
  12.5 9.8 %all-to-all-start.1 = ((f32[16,48,128]{2,1,0:T(8,128)}), f32[16,48,128]{2,1,0:T(8,128)S(1)}, u32[]{:S(2)}, u32[]{:S(2)}) async-start(f32[16,48,128]{2,1,0:T(8,128)} %broadcast_in_dim.5), calls=%async_computation.1 | async-start | bytes 786432 | tf_op jit(solution)/shard_map/all_to_all | solution.py:18
  22.3 5.0 %copy.46 = f32[48,512,16]{0,2,1:T(8,128)} copy(f32[48,512,16]{1,2,0:T(8,128)} %copy-done.2) | data formatting | bytes 3145728 | tf_op jit(solution)/shard_map/mul | solution.py:47
  27.3 3.7 %copy.47 = f32[48,16,512]{2,0,1:T(8,128)} copy(f32[48,16,512]{0,2,1:T(8,128)} %bitcast.40) | data formatting | bytes 3145728 | tf_op jit(solution)/shard_map/reshape | solution.py:48
  31.0 5.0 %all-to-all-done.1 = f32[16,48,128]{2,1,0:T(8,128)S(1)} async-done(((f32[16,48,128]{2,1,0:T(8,128)}), f32[16,48,128]{2,1,0:T(8,128)S(1)}, u32[]{:S(2)}, u32[]{:S(2)}) %all-to-all-start.1) | async-done | bytes 393248 | tf_op jit(solution)/shard_map/all_to_all | solution.py:18
  36.0 4.4 %all-to-all-start = ((f32[48,16,512]{2,0,1:T(8,128)}), f32[48,16,512]{2,0,1:T(8,128)}, u32[]{:S(2)}, u32[]{:S(2)}) async-start(f32[48,16,512]{2,0,1:T(8,128)} %copy.47), calls=%async_computation | async-start | bytes 3145728 | tf_op jit(solution)/shard_map/all_to_all | solution.py:49
  40.4 0.0 reduce-scatter.7.cloned.1.call-start
  40.4 2.8 reshape.59
  43.2 0.3 copy.51
  43.6 3.0 fusion.3
  46.6 32.0 %all-to-all-done = f32[48,16,512]{2,0,1:T(8,128)} async-done(((f32[48,16,512]{2,0,1:T(8,128)}), f32[48,16,512]{2,0,1:T(8,128)}, u32[]{:S(2)}, u32[]{:S(2)}) %all-to-all-start) | async-done | bytes 1572896 | tf_op jit(solution)/shard_map/all_to_all | solution.py:49
  78.6 0.0 copy-done
  78.6 4.1 %convolution_multiply_fusion = f32[768,1024]{1,0:T(8,128)S(1)} fusion(f32[768,512]{1,0:T(8,128)} %bitcast.4, f32[512,1024]{1,0:T(8,128)S(1)} %bitcast.39), kind=kOutput, calls=%fused_computation | convolution fusion | flops 2416705536 | bytes 6815744 | tf_op jit(solution)/shard_map/dot_general | solution.py:51
  82.8 0.0 copy-start.1
  82.8 1.7 copy-done.1
  84.4 0.1 constant_dynamic-slice_fusion
  84.5 0.1 copy_add_fusion
  84.7 0.1 copy.56
  84.8 3.6 %dynamic_update_slice.3 = f32[16,48,1024]{2,1,0:T(8,128)} dynamic-update-slice(f32[16,48,1024]{2,1,0:T(8,128)} %bitcast.42, f32[16,3,1024]{2,1,0:T(4,128)S(1)} %copy.56, s32[]{:T(128)} %constant.5.clone.1, s32[]{:T(128)S(6)} %select_n.14, s32[]{:T(128)} %constant.5.clone.1) | dynamic-update-slice | bytes 393220 | tf_op jit(solution)/shard_map/dynamic_update_slice | solution.py:75
  88.4 3.5 %copy.64 = f32[768,1024]{0,1:T(8,128)} copy(f32[768,1024]{1,0:T(8,128)} %bitcast.43) | data formatting | bytes 6291456
  92.0 0.0 copy-start.4
  92.0 0.0 slice-start
  92.0 0.0 slice-start.1
  92.0 0.0 reduce-scatter.7.cloned.1.call-update
  92.0 0.0 reduce-scatter.9.cloned.1.call-start
  92.0 0.6 copy-done.4
  92.6 0.6 dynamic_slice.14
  93.2 0.0 slice-done
  93.2 0.0 slice-done.1
  93.2 0.1 add_bitcast_fusion
  93.3 0.1 dynamic_slice.15
  93.3 141.1 %reduce-scatter.7.cloned.1.call-done = f32[32,768]{1,0:T(8,128)} async-done(((f32[1024,768]{1,0:T(8,128)}), f32[32,768]{1,0:T(8,128)}) %reduce-scatter.7.cloned.1.call-update) | async-done | bytes 98320
  234.4 1.8 copy.66
  236.2 0.0 reduce-scatter.9.cloned.1.call-update
  236.3 0.7 broadcast_add_fusion
  236.9 83.5 %reduce-scatter.9.cloned.1.call-done = f32[48,32]{1,0:T(8,128)} async-done(((f32[768,32]{1,0:T(8,128)}), f32[48,32]{1,0:T(8,128)}) %reduce-scatter.9.cloned.1.call-update) | async-done | bytes 6160
  320.4 0.8 copy.67
  321.2 0.0 copy-done.3
  321.2 0.7 divide_multiply_fusion
  (3 shorter events, 0.1 us)
Async XLA Ops:
  6.5 72.1 %copy-start = (f32[32,16,1024]{2,1,0:T(8,128)S(1)}, f32[32,16,1024]{2,1,0:T(8,128)}, u32[]{:S(2)}) copy-start(f32[32,16,1024]{2,1,0:T(8,128)} %param.9) | copy-start | bytes 6291460
  10.2 1.2 copy-start.2
  12.5 23.5 %all-to-all-start.1 = ((f32[16,48,128]{2,1,0:T(8,128)}), f32[16,48,128]{2,1,0:T(8,128)S(1)}, u32[]{:S(2)}, u32[]{:S(2)}) async-start(f32[16,48,128]{2,1,0:T(8,128)} %broadcast_in_dim.5), calls=%async_computation.1 | async-start | bytes 786432 | tf_op jit(solution)/shard_map/all_to_all | solution.py:18
  36.0 42.6 %all-to-all-start = ((f32[48,16,512]{2,0,1:T(8,128)}), f32[48,16,512]{2,0,1:T(8,128)}, u32[]{:S(2)}, u32[]{:S(2)}) async-start(f32[48,16,512]{2,0,1:T(8,128)} %copy.47), calls=%async_computation | async-start | bytes 3145728 | tf_op jit(solution)/shard_map/all_to_all | solution.py:49
  40.4 194.0 %reduce-scatter.7.cloned.1.call-start = ((), (), s32[]{:S(2)}) async-start(), calls=%async_computation.4 | async-start | bytes 3244032
  82.8 1.7 copy-start.1
  92.0 0.7 copy-start.4
  92.0 1.2 slice-start
  92.0 1.2 slice-start.1
  92.0 229.3 %copy-start.3 = (f32[48,32]{0,1:T(8,128)S(1)}, f32[48,32]{0,1:T(8,128)}, u32[]{:S(2)}) copy-start(f32[48,32]{0,1:T(8,128)} %param.11) | copy-start | bytes 18436
  92.0 228.4 %reduce-scatter.9.cloned.1.call-start = ((), (), s32[]{:S(2)}) async-start(), calls=%async_computation.5 | async-start | bytes 417792
Sparse Core Ops, SparseCore 0:
  92.1 142.2 reduce-scatter.6
  237.2 83.1 reduce-scatter.8

commit v2 on v1

v2 whole, which is shorter than its diff:
```python
import jax
import jax.numpy as jnp
from jax import lax
from jax.experimental import pallas as pl
from jax.experimental.pallas import tpu as pltpu
from jax.sharding import PartitionSpec as P

OCCUPIED = 48
VIRTUAL = 512
A_WINDOW = 8
B_WINDOW = 128
X = 4
Z_LOW = 4
Z_HIGH = 2
Y = 8
OWNERS = X * Z_LOW
LANES = 128
C_SHARE = VIRTUAL // OWNERS
D_SHARE = 16
DEPTH = C_SHARE * D_SHARE
J_SHARE = OCCUPIED // OWNERS
COL_SHARE = 32
CHUNKS = ((0, 16), (16, 16), (32, 8), (40, 8))
MESH = pl.DeviceIdType.MESH
F32 = jnp.float32
BF16 = jnp.bfloat16


def halves(value):
    high = value.astype(BF16)
    low = (value - high.astype(F32)).astype(BF16)
    return high, low


def product(left, right):
    (lh, ll), (rh, rl) = left, right
    out = jnp.dot(lh, rl, preferred_element_type=F32)
    out += jnp.dot(ll, rh, preferred_element_type=F32)
    return out + jnp.dot(lh, rh, preferred_element_type=F32)


def settle(ref, sem):
    pltpu.make_async_copy(ref, ref, sem).wait()


def kernel(
    live_ref, occ_ref, vir_ref, t_hbm, w_hbm, u_hbm, pair_ref, out_ref,
    t_v, w_v, u_v, wh, wl, uh, ul, send_t, cyc_own, cyc_all, cyc_out, final, turned,
    local_sem, cyc_sem, t_send, t_recv, core_send, core_recv, y_send, y_recv, p_send, p_recv,
    f_send, f_recv, *bufs,
):
    n = len(CHUNKS)
    recv_t, grid, core_in, y_in, y_out, plane_in = (bufs[k * n : (k + 1) * n] for k in range(6))
    occ = lax.axis_index("occ")
    sec = lax.axis_index("sec")
    x, zl = occ // Z_LOW, occ % Z_LOW
    zh, y, core = sec // 16, (sec // 2) % Y, sec % 2
    half = y % 2
    slot = (occ % 2) * 8 + occ // 2
    holder = jnp.logical_and(zl % 2 == half, zh == core)
    live = live_ref[occ]

    copies = []
    for k in range(X):
        copies.append(
            pltpu.make_async_copy(
                t_hbm.at[:, pl.ds(k * LANES, LANES)], t_v.at[k], local_sem.at[0]
            )
        )
        copies[-1].start()
    for k in range(A_WINDOW):
        pltpu.make_async_copy(
            w_hbm.at[:, pl.ds(k * LANES, LANES)], w_v.at[k], local_sem.at[1]
        ).start()
    pltpu.make_async_copy(u_hbm, u_v, local_sem.at[2]).start()

    barrier = pltpu.get_barrier_semaphore()

    def greet(o, s):
        pl.semaphore_signal(barrier, inc=1, device_id={"occ": o, "sec": s}, device_id_type=MESH)

    def greet_occ(k, carry):
        greet((occ + k) % OWNERS, sec)
        return carry

    def greet_far(k, carry):
        greet((occ + k) % OWNERS, (sec + 16) % 32)
        return carry

    def greet_y(k, carry):
        greet(occ, zh * 16 + ((y + k) % Y) * 2 + core)
        return carry

    lax.fori_loop(1, OWNERS, greet_occ, 0)
    lax.fori_loop(0, OWNERS, greet_far, 0)
    lax.fori_loop(1, Y, greet_y, 0)
    y_twin = y + 1 - 2 * half
    same_y = zh * 16 + y * 2
    twin_y = zh * 16 + y_twin * 2
    greet(occ, same_y + 1 - core)
    greet(occ, twin_y + 1 - core)

    lane_group = lax.broadcasted_iota(jnp.int32, (8, LANES), 1) // C_SHARE
    sub_row = lax.broadcasted_iota(jnp.int32, (8, LANES), 0)

    def relay(r0, rows):
        def tile(k, carry):
            for b in range(rows // 8):
                p0 = r0 + 8 * b
                keep = sub_row + p0 < live
                for g in range(4):
                    part = [
                        jnp.where(keep, t_v[k, pl.ds(p0 * D_SHARE + 4 * g + d, 8, stride=D_SHARE), :], 0.0)
                        for d in range(4)
                    ]
                    for z in range(Z_LOW):
                        row = None
                        for d in range(4):
                            shift = ((d - z) * C_SHARE) % LANES
                            turn = pltpu.roll(part[d], shift, 1) if shift else part[d]
                            row = turn if row is None else jnp.where(lane_group == d, turn, row)
                        send_t[k * Z_LOW + z, p0 : p0 + 8, g * LANES : (g + 1) * LANES] = row
            return carry

        lax.fori_loop(0, X, tile, 0)

    def send_rows(t):
        r0, rows = CHUNKS[t]

        def one(k, carry):
            o = (occ + k) % OWNERS
            pltpu.make_async_remote_copy(
                src_ref=send_t.at[o, pl.ds(r0, rows)],
                dst_ref=recv_t[t].at[slot],
                send_sem=t_send.at[t],
                recv_sem=t_recv.at[t],
                device_id={"occ": o, "sec": sec},
                device_id_type=MESH,
            ).start()
            return carry

        lax.fori_loop(1, OWNERS, one, 0)
        recv_t[t][slot] = send_t[occ, r0 : r0 + rows, :]

    settle(t_v, local_sem.at[0])
    for q in range(OCCUPIED * D_SHARE // LANES):
        rows = lax.broadcasted_iota(jnp.int32, (LANES, LANES), 0) // D_SHARE + q * (LANES // D_SHARE)
        block = jnp.where(rows < live, t_v[0, q * LANES : (q + 1) * LANES, :], 0.0)
        cyc_own[:, q * LANES : (q + 1) * LANES] = block.T[:A_WINDOW, :]
    relay(*CHUNKS[0])
    pl.semaphore_wait(barrier, 40)

    def cyc_z(k, carry):
        pltpu.make_async_remote_copy(
            src_ref=cyc_own,
            dst_ref=cyc_all.at[occ],
            send_sem=cyc_sem.at[0],
            recv_sem=cyc_sem.at[1],
            device_id={"occ": x * Z_LOW + (zl + k) % Z_LOW, "sec": sec},
            device_id_type=MESH,
        ).start()
        return carry

    lax.fori_loop(1, Z_LOW, cyc_z, 0)
    cyc_all[occ] = cyc_own[...]
    send_rows(0)
    relay(*CHUNKS[1])
    send_rows(1)

    settle(cyc_all.at[pl.ds(0, Z_LOW - 1)], cyc_sem.at[1])

    def cyc_x(k, carry):
        mine = cyc_all.at[pl.ds(x * Z_LOW, Z_LOW)]
        pltpu.make_async_remote_copy(
            src_ref=mine,
            dst_ref=mine,
            send_sem=cyc_sem.at[2],
            recv_sem=cyc_sem.at[3],
            device_id={"occ": ((x + k) % X) * Z_LOW + zl, "sec": sec},
            device_id_type=MESH,
        ).start()
        return carry

    lax.fori_loop(1, X, cyc_x, 0)
    for t in range(2, n):
        relay(*CHUNKS[t])

    settle(w_v, local_sem.at[1])

    def weights(a, carry):
        col = pl.multiple_of(((a % 4) * 2 + a // 4) * LANES, LANES)
        for d in range(D_SHARE):
            high, low = halves(w_v[a, pl.ds(d, C_SHARE, stride=D_SHARE), :])
            wh[d * C_SHARE : (d + 1) * C_SHARE, pl.ds(col, LANES)] = high
            wl[d * C_SHARE : (d + 1) * C_SHARE, pl.ds(col, LANES)] = low
        return carry

    lax.fori_loop(0, A_WINDOW, weights, 0)
    settle(u_v, local_sem.at[2])
    for k in range(0, OCCUPIED * D_SHARE, LANES):
        uh[k : k + LANES, :], ul[k : k + LANES, :] = halves(u_v[k : k + LANES, :])

    settle(cyc_all.at[pl.ds(0, OWNERS - Z_LOW)], cyc_sem.at[3])
    settle(cyc_own, cyc_sem.at[0])
    settle(cyc_own, cyc_sem.at[0])
    settle(cyc_own, cyc_sem.at[0])
    settle(cyc_all.at[pl.ds(0, OWNERS - Z_LOW)], cyc_sem.at[2])
    rows_cyc = halves(cyc_all[...].reshape(OWNERS * A_WINDOW, OCCUPIED * D_SHARE))
    cyc = product(rows_cyc, (uh[...], ul[...]))
    for jj in range(J_SHARE):
        cyc_out[jj] = cyc[:, jj * LANES : (jj + 1) * LANES]

    wide = lax.broadcasted_iota(jnp.int32, (COL_SHARE, OCCUPIED), 1)
    tall = lax.broadcasted_iota(jnp.int32, (COL_SHARE, OCCUPIED), 0)
    sub = half * 2 + core
    occ_pair = lax.fori_loop(
        0, OCCUPIED, lambda j, v: jnp.where(wide == j, occ_ref[occ] + occ_ref[j], v),
        jnp.zeros((COL_SHARE, OCCUPIED), F32),
    )
    vir_pair = lax.fori_loop(
        0, COL_SHARE,
        lambda b, v: jnp.where(tall == b, vir_ref[zh * 4 + y // 2] + vir_ref[sub * COL_SHARE + b], v),
        jnp.zeros((COL_SHARE, OCCUPIED), F32),
    )
    bottom = occ_pair - vir_pair
    alive = (wide < live).astype(F32)

    def ladder(t):
        r0, rows = CHUNKS[t]
        left = halves(recv_t[t][...].reshape(OWNERS * rows, DEPTH))
        for al in range(4):
            cols = slice(al * 2 * LANES, (al + 1) * 2 * LANES)
            out = 0.5 * product(left, (wh[:, cols], wl[:, cols]))
            grid[t][0, al] = out[:, :LANES].reshape(2, 8 * rows, LANES)
            grid[t][1, al] = out[:, LANES:].reshape(2, 8 * rows, LANES)
        for jj in range(J_SHARE):
            row = occ * J_SHARE + jj - r0

            @pl.when(jnp.logical_and(row >= 0, row < rows))
            def _():
                for a in range(A_WINDOW):
                    for e in range(2):
                        here = (a // 4, a % 4, e, pl.ds(row, 8, stride=rows), slice(None))
                        grid[t][here] += cyc_out[jj, pl.ds(e * A_WINDOW + a, 8, stride=2 * A_WINDOW), :]

    def core_copy(t):
        return pltpu.make_async_remote_copy(
            src_ref=grid[t].at[1 - core],
            dst_ref=core_in[t],
            send_sem=core_send.at[t],
            recv_sem=core_recv.at[t],
            device_id={"occ": occ, "sec": same_y + 1 - core},
            device_id_type=MESH,
        )

    def along_y(t):
        core_copy(t).wait()
        grid[t][core] += core_in[t][...]

        def one(k, carry):
            to = (y + k) % Y
            pltpu.make_async_remote_copy(
                src_ref=grid[t].at[core, to // 2, to % 2],
                dst_ref=y_in[t].at[y],
                send_sem=y_send.at[t],
                recv_sem=y_recv.at[t],
                device_id={"occ": occ, "sec": zh * 16 + to * 2 + core},
                device_id_type=MESH,
            ).start()
            return carry

        lax.fori_loop(1, Y, one, 0)

    my_pair = occ // 2

    def across_plane(t):
        r0, rows = CHUNKS[t]
        settle(y_in[t].at[pl.ds(0, Y - 1)], y_recv.at[t])
        settle(y_in[t].at[pl.ds(0, Y - 1)], y_send.at[t])
        total = grid[t][core, y // 2, half]
        for k in range(1, Y):
            total += y_in[t][(y + k) % Y]
        y_out[t][...] = total.reshape(8, rows, LANES)

        def one(k, carry):
            @pl.when(jnp.logical_not(jnp.logical_and(holder, k == my_pair)))
            def _():
                pltpu.make_async_remote_copy(
                    src_ref=y_out[t].at[k],
                    dst_ref=plane_in[t].at[zh * OWNERS + occ],
                    send_sem=p_send.at[t],
                    recv_sem=p_recv.at[t],
                    device_id={
                        "occ": (k // 2) * Z_LOW + (k % 2) * 2 + half,
                        "sec": core * 16 + y * 2 + core,
                    },
                    device_id_type=MESH,
                ).start()

            return carry

        lax.fori_loop(0, 8, one, 0)

        @pl.when(holder)
        def _():
            plane_in[t][zh * OWNERS + occ] = y_out[t][my_pair]

    for t in range(n):
        settle(recv_t[t].at[pl.ds(0, OWNERS - 1)], t_recv.at[t])
        if t + 2 < n:
            send_rows(t + 2)
        ladder(t)
        core_copy(t).start()
        if t > 0:
            across_plane(t - 1)
        along_y(t)
    across_plane(n - 1)

    group = (
        {"occ": occ, "sec": same_y + 1 - core},
        {"occ": occ, "sec": twin_y + core},
        {"occ": occ, "sec": twin_y + 1 - core},
    )

    @pl.when(holder)
    def _():
        for t, (r0, rows) in enumerate(CHUNKS):
            settle(plane_in[t].at[pl.ds(0, 31)], p_recv.at[t])
            settle(y_out[t].at[pl.ds(0, 7)], p_send.at[t])
            total = plane_in[t][0]
            for k in range(1, 32):
                total += plane_in[t][k]
            final[r0 : r0 + rows, :] = total
        outs = [
            pltpu.make_async_remote_copy(
                src_ref=final,
                dst_ref=final,
                send_sem=f_send.at[k],
                recv_sem=f_recv,
                device_id=to,
                device_id_type=MESH,
            )
            for k, to in enumerate(group)
        ]
        for copy in outs:
            copy.start()
        for copy in outs:
            copy.wait_send()

    @pl.when(jnp.logical_not(holder))
    def _():
        for t in range(n):
            settle(y_out[t], p_send.at[t])
        settle(final, f_recv)

    turned[...] = final[...].T
    summed = turned[pl.ds(pl.multiple_of(sub * COL_SHARE, COL_SHARE), COL_SHARE), :]
    out_ref[...] = (summed + pair_ref[...]) / bottom * alive

    for t, (r0, rows) in enumerate(CHUNKS):
        settle(send_t.at[pl.ds(0, OWNERS - 1), pl.ds(r0, rows)], t_send.at[t])


def shards(amplitudes, live_pairs, ladder_ints, cycle_ints, pair_ints, occ_energy, vir_energy):
    n = len(CHUNKS)
    smem = pl.BlockSpec(memory_space=pltpu.SMEM)
    vmem = pl.BlockSpec(memory_space=pltpu.VMEM)
    anywhere = pl.BlockSpec(memory_space=pl.ANY)
    dma = pltpu.SemaphoreType.DMA
    rows = [r for _, r in CHUNKS]
    scratch = [
        pltpu.VMEM((X, OCCUPIED * D_SHARE, LANES), F32),
        pltpu.VMEM((A_WINDOW, DEPTH, LANES), F32),
        pltpu.VMEM((OCCUPIED * D_SHARE, J_SHARE * LANES), F32),
        pltpu.VMEM((DEPTH, A_WINDOW * LANES), BF16),
        pltpu.VMEM((DEPTH, A_WINDOW * LANES), BF16),
        pltpu.VMEM((OCCUPIED * D_SHARE, J_SHARE * LANES), BF16),
        pltpu.VMEM((OCCUPIED * D_SHARE, J_SHARE * LANES), BF16),
        pltpu.VMEM((OWNERS, OCCUPIED, DEPTH), F32),
        pltpu.VMEM((A_WINDOW, OCCUPIED * D_SHARE), F32),
        pltpu.VMEM((OWNERS, A_WINDOW, OCCUPIED * D_SHARE), F32),
        pltpu.VMEM((J_SHARE, OWNERS * A_WINDOW, LANES), F32),
        pltpu.VMEM((OCCUPIED, LANES), F32),
        pltpu.VMEM((LANES, OCCUPIED), F32),
        dma((3,)),
        dma((4,)),
        dma((n,)),
        dma((n,)),
        dma((n,)),
        dma((n,)),
        dma((n,)),
        dma((n,)),
        dma((n,)),
        dma((n,)),
        dma((3,)),
        dma,
    ]
    scratch += [pltpu.VMEM((OWNERS, r, DEPTH), F32) for r in rows]
    scratch += [pltpu.VMEM((2, 4, 2, 8 * r, LANES), F32) for r in rows]
    scratch += [pltpu.VMEM((4, 2, 8 * r, LANES), F32) for r in rows]
    scratch += [pltpu.VMEM((Y, 8 * r, LANES), F32) for r in rows]
    scratch += [pltpu.VMEM((8, r, LANES), F32) for r in rows]
    scratch += [pltpu.VMEM((32, r, LANES), F32) for r in rows]
    out = pl.pallas_call(
        kernel,
        out_shape=jax.ShapeDtypeStruct((COL_SHARE, OCCUPIED), F32),
        in_specs=[smem, smem, smem, anywhere, anywhere, anywhere, vmem],
        out_specs=vmem,
        scratch_shapes=scratch,
        compiler_params=pltpu.CompilerParams(
            collective_id=0, has_side_effects=True, vmem_limit_bytes=48 * 1024 * 1024
        ),
    )(
        live_pairs,
        occ_energy,
        vir_energy,
        amplitudes.transpose(0, 2, 1).reshape(OCCUPIED * D_SHARE, VIRTUAL),
        ladder_ints.reshape(DEPTH, A_WINDOW * B_WINDOW),
        cycle_ints.reshape(OCCUPIED * D_SHARE, J_SHARE * B_WINDOW),
        pair_ints.T,
    )
    return out.T


def solution(mesh):
    in_specs = (
        P("occ", None, "sec"),
        P(),
        P("occ", "sec", None),
        P(None, "sec", "occ"),
        P("occ", "sec"),
        P(),
        P(),
    )
    return jax.shard_map(shards, mesh=mesh, in_specs=in_specs, out_specs=P("occ", "sec"), check_vma=False)
```

time: 329 us -> 106 us (0.32)
  the two profiles are of different devices: /device:TPU:8 before, /device:TPU:1 now
where the time goes in v2:
time: 106 us; the launch traced here: 105 us
  Pallas kernels  97.5 us (92%)
  local copies, waits for them, and re-layouts  7.58 us (7%)
    pallas_call x1, Pallas kernels, shards(): pl.pallas_call(kernel, out_shape=jax.ShapeDtypeStruct((COL_SHARE, OCCUPIE...  97.5 us
    unnamed x15, local copies, waits for them, and re-layouts  7.58 us

profile of v2, /device:TPU:1, one launch (start us, length us, event | category | flops | bytes accessed | tf_op | source)
XLA Modules:
  0.0 105.1 jit_solution(2155485721244427006)
XLA Ops:
  0.0 0.0 copy-start
  0.0 1.6 %copy-done = f32[32,16,1024]{2,1,0:T(8,128)S(1)} copy-done((f32[32,16,1024]{2,1,0:T(8,128)S(1)}, f32[32,16,1024]{2,1,0:T(8,128)}, u32[]{:S(2)}) %copy-start) | copy-done | bytes 2097176
  1.6 0.0 copy-start.1
  1.6 1.4 %copy-done.1 = f32[48,512,16]{1,2,0:T(8,128)S(1)} copy-done((f32[48,512,16]{1,2,0:T(8,128)S(1)}, f32[48,512,16]{1,2,0:T(8,128)}, u32[]{:S(2)}) %copy-start.1) | copy-done | bytes 1572888
  3.0 0.0 copy-start.2
  3.0 1.3 %copy-done.2 = f32[48,16,384]{2,1,0:T(8,128)S(1)} copy-done((f32[48,16,384]{2,1,0:T(8,128)S(1)}, f32[48,16,384]{2,1,0:T(8,128)}, u32[]{:S(2)}) %copy-start.2) | copy-done | bytes 1179672
  4.3 0.0 copy-start.3
  4.3 0.7 copy-done.3
  5.0 0.0 copy-start.4
  5.0 0.7 copy-done.4
  5.7 0.0 copy-start.5
  5.7 0.7 copy-done.5
  6.3 0.0 copy-start.6
  6.3 0.7 copy-done.6
  7.0 97.5 %shard_map.73 = f32[32,48]{1,0:T(8,128)S(1)} custom-call(s32[16]{0:T(128)S(1)} %copy-done.5, f32[48]{0:T(128)S(1)} %copy-done.6, f32[512]{0:T(512)S(1)} %copy-done.4, f32[768,512]{1,0:T(8,128)S(1)} %bitcast.8, f32[512,1024]{1,0:T(8,128)S(1)} %bitcast.7, f32[768,384]{1,0:T(8,128)S(1)} %bitcast.9, f32[32,48]{1,0:T(8,128)S(1)} %bitcast.11), custom_call_target="tpu_custom_call" | custom-call | tf_op jit(solution)/shard_map/pallas_call | solution.py:404
  104.5 0.6 copy.9
Async XLA Ops:
  0.0 1.6 %copy-start = (f32[32,16,1024]{2,1,0:T(8,128)S(1)}, f32[32,16,1024]{2,1,0:T(8,128)}, u32[]{:S(2)}) copy-start(f32[32,16,1024]{2,1,0:T(8,128)} %param.9) | copy-start | bytes 6291460
  1.6 1.4 %copy-start.1 = (f32[48,512,16]{1,2,0:T(8,128)S(1)}, f32[48,512,16]{1,2,0:T(8,128)}, u32[]{:S(2)}) copy-start(f32[48,512,16]{1,2,0:T(8,128)} %param.7) | copy-start | bytes 4718596
  3.0 1.3 %copy-start.2 = (f32[48,16,384]{2,1,0:T(8,128)S(1)}, f32[48,16,384]{2,1,0:T(8,128)}, u32[]{:S(2)}) copy-start(f32[48,16,384]{2,1,0:T(8,128)} %param.10) | copy-start | bytes 3538948
  4.3 0.7 copy-start.3
  5.0 0.7 copy-start.4
  5.7 0.7 copy-start.5
  6.3 0.7 copy-start.6

commit v3 on v2

--- a/solution.py
+++ b/solution.py
@@ -20,7 +20,7 @@
 DEPTH = C_SHARE * D_SHARE
 J_SHARE = OCCUPIED // OWNERS
 COL_SHARE = 32
-CHUNKS = ((0, 16), (16, 16), (32, 8), (40, 8))
+CHUNKS = tuple((8 * t, 8) for t in range(6))
 MESH = pl.DeviceIdType.MESH
 F32 = jnp.float32
 BF16 = jnp.bfloat16
@@ -44,9 +44,9 @@
 
 
 def kernel(
-    live_ref, occ_ref, vir_ref, t_hbm, w_hbm, u_hbm, pair_ref, out_ref,
-    t_v, w_v, u_v, wh, wl, uh, ul, send_t, cyc_own, cyc_all, cyc_out, final, turned,
-    local_sem, cyc_sem, t_send, t_recv, core_send, core_recv, y_send, y_recv, p_send, p_recv,
+    live_hbm, occ_hbm, vir_hbm, t_hbm, w_hbm, u_hbm, pair_hbm, out_ref,
+    live_ref, occ_ref, vir_ref, pair_ref, t_v, w_v, u_v, w3, t3, uh, ul, send_t, cyc_own, cyc_all, cyc_out, final, turned,
+    local_sem, cyc_sem, t_send, t_recv, core_send, core_recv, y_send, y_mid, y_recv, p_send, p_recv,
     f_send, f_recv, *bufs,
 ):
     n = len(CHUNKS)
@@ -58,21 +58,25 @@
     half = y % 2
     slot = (occ % 2) * 8 + occ // 2
     holder = jnp.logical_and(zl % 2 == half, zh == core)
-    live = live_ref[occ]
-
-    copies = []
+
+    live_copy = pltpu.make_async_copy(live_hbm, live_ref, local_sem.at[3])
+    live_copy.start()
     for k in range(X):
-        copies.append(
-            pltpu.make_async_copy(
-                t_hbm.at[:, pl.ds(k * LANES, LANES)], t_v.at[k], local_sem.at[0]
-            )
-        )
-        copies[-1].start()
+        pltpu.make_async_copy(
+            t_hbm.at[:, pl.ds(k * LANES, LANES)], t_v.at[k], local_sem.at[0]
+        ).start()
     for k in range(A_WINDOW):
         pltpu.make_async_copy(
             w_hbm.at[:, pl.ds(k * LANES, LANES)], w_v.at[k], local_sem.at[1]
         ).start()
     pltpu.make_async_copy(u_hbm, u_v, local_sem.at[2]).start()
+    small = (
+        pltpu.make_async_copy(occ_hbm, occ_ref, local_sem.at[4]),
+        pltpu.make_async_copy(vir_hbm, vir_ref, local_sem.at[5]),
+        pltpu.make_async_copy(pair_hbm, pair_ref, local_sem.at[6]),
+    )
+    for copy in small:
+        copy.start()
 
     barrier = pltpu.get_barrier_semaphore()
 
@@ -142,6 +146,8 @@
         lax.fori_loop(1, OWNERS, one, 0)
         recv_t[t][slot] = send_t[occ, r0 : r0 + rows, :]
 
+    live_copy.wait()
+    live = live_ref[occ]
     settle(t_v, local_sem.at[0])
     for q in range(OCCUPIED * D_SHARE // LANES):
         rows = lax.broadcasted_iota(jnp.int32, (LANES, LANES), 0) // D_SHARE + q * (LANES // D_SHARE)
@@ -184,6 +190,7 @@
     lax.fori_loop(1, X, cyc_x, 0)
     for t in range(2, n):
         relay(*CHUNKS[t])
+        send_rows(t)
 
     settle(w_v, local_sem.at[1])
 
@@ -191,8 +198,8 @@
         col = pl.multiple_of(((a % 4) * 2 + a // 4) * LANES, LANES)
         for d in range(D_SHARE):
             high, low = halves(w_v[a, pl.ds(d, C_SHARE, stride=D_SHARE), :])
-            wh[d * C_SHARE : (d + 1) * C_SHARE, pl.ds(col, LANES)] = high
-            wl[d * C_SHARE : (d + 1) * C_SHARE, pl.ds(col, LANES)] = low
+            for k, half_of in enumerate((low, high, high)):
+                w3[k * DEPTH + d * C_SHARE : k * DEPTH + (d + 1) * C_SHARE, pl.ds(col, LANES)] = half_of
         return carry
 
     lax.fori_loop(0, A_WINDOW, weights, 0)
@@ -201,15 +208,15 @@
         uh[k : k + LANES, :], ul[k : k + LANES, :] = halves(u_v[k : k + LANES, :])
 
     settle(cyc_all.at[pl.ds(0, OWNERS - Z_LOW)], cyc_sem.at[3])
-    settle(cyc_own, cyc_sem.at[0])
-    settle(cyc_own, cyc_sem.at[0])
-    settle(cyc_own, cyc_sem.at[0])
+    settle(cyc_all.at[pl.ds(0, Z_LOW - 1)], cyc_sem.at[0])
     settle(cyc_all.at[pl.ds(0, OWNERS - Z_LOW)], cyc_sem.at[2])
     rows_cyc = halves(cyc_all[...].reshape(OWNERS * A_WINDOW, OCCUPIED * D_SHARE))
     cyc = product(rows_cyc, (uh[...], ul[...]))
     for jj in range(J_SHARE):
         cyc_out[jj] = cyc[:, jj * LANES : (jj + 1) * LANES]
 
+    for copy in small:
+        copy.wait()
     wide = lax.broadcasted_iota(jnp.int32, (COL_SHARE, OCCUPIED), 1)
     tall = lax.broadcasted_iota(jnp.int32, (COL_SHARE, OCCUPIED), 0)
     sub = half * 2 + core
@@ -225,61 +232,98 @@
     bottom = occ_pair - vir_pair
     alive = (wide < live).astype(F32)
 
-    def ladder(t):
-        r0, rows = CHUNKS[t]
-        left = halves(recv_t[t][...].reshape(OWNERS * rows, DEPTH))
-        for al in range(4):
-            cols = slice(al * 2 * LANES, (al + 1) * 2 * LANES)
-            out = 0.5 * product(left, (wh[:, cols], wl[:, cols]))
-            grid[t][0, al] = out[:, :LANES].reshape(2, 8 * rows, LANES)
-            grid[t][1, al] = out[:, LANES:].reshape(2, 8 * rows, LANES)
-        for jj in range(J_SHARE):
-            row = occ * J_SHARE + jj - r0
-
-            @pl.when(jnp.logical_and(row >= 0, row < rows))
-            def _():
-                for a in range(A_WINDOW):
-                    for e in range(2):
-                        here = (a // 4, a % 4, e, pl.ds(row, 8, stride=rows), slice(None))
-                        grid[t][here] += cyc_out[jj, pl.ds(e * A_WINDOW + a, 8, stride=2 * A_WINDOW), :]
-
-    def core_copy(t):
+    def core_piece(t, al):
         return pltpu.make_async_remote_copy(
-            src_ref=grid[t].at[1 - core],
-            dst_ref=core_in[t],
+            src_ref=grid[t].at[1 - core, al],
+            dst_ref=core_in[t].at[al],
             send_sem=core_send.at[t],
             recv_sem=core_recv.at[t],
             device_id={"occ": occ, "sec": same_y + 1 - core},
             device_id_type=MESH,
         )
 
-    def along_y(t):
-        core_copy(t).wait()
+    def ladder(t):
+        settle(recv_t[t].at[pl.ds(0, OWNERS - 1)], t_recv.at[t])
+        r0, rows = CHUNKS[t]
+        high, low = halves(recv_t[t][...].reshape(OWNERS * rows, DEPTH))
+        left = t3.at[pl.ds(0, OWNERS * rows)]
+        left[:, :DEPTH] = high
+        left[:, DEPTH : 2 * DEPTH] = low
+        left[:, 2 * DEPTH :] = high
+        for al in range(4):
+            cols = slice(al * 2 * LANES, (al + 1) * 2 * LANES)
+            out = 0.5 * jnp.dot(left[...], w3[:, cols], preferred_element_type=F32)
+            grid[t][0, al] = out[:, :LANES].reshape(2, 8 * rows, LANES)
+            grid[t][1, al] = out[:, LANES:].reshape(2, 8 * rows, LANES)
+            for jj in range(J_SHARE):
+                row = occ * J_SHARE + jj - r0
+
+                @pl.when(jnp.logical_and(row >= 0, row < rows))
+                def _():
+                    for ah in range(2):
+                        for e in range(2):
+                            here = (ah, al, e, pl.ds(row, 8, stride=rows), slice(None))
+                            a = ah * 4 + al
+                            grid[t][here] += cyc_out[jj, pl.ds(e * A_WINDOW + a, 8, stride=2 * A_WINDOW), :]
+
+            core_piece(t, al).start()
+
+    def ship(src, dst, send, recv, to):
+        pltpu.make_async_remote_copy(
+            src_ref=src,
+            dst_ref=dst,
+            send_sem=send,
+            recv_sem=recv,
+            device_id={"occ": occ, "sec": zh * 16 + to * 2 + core},
+            device_id_type=MESH,
+        ).start()
+
+    def portion(t, to):
+        return grid[t].at[core, to // 2, to % 2]
+
+    steps = ((0, 1), (1, Y - 1))
+
+    def first_round(t):
+        settle(core_in[t], core_recv.at[t])
         grid[t][core] += core_in[t][...]
-
-        def one(k, carry):
-            to = (y + k) % Y
-            pltpu.make_async_remote_copy(
-                src_ref=grid[t].at[core, to // 2, to % 2],
-                dst_ref=y_in[t].at[y],
-                send_sem=y_send.at[t],
-                recv_sem=y_recv.at[t],
-                device_id={"occ": occ, "sec": zh * 16 + to * 2 + core},
-                device_id_type=MESH,
-            ).start()
-            return carry
-
-        lax.fori_loop(1, Y, one, 0)
+        part = 4 * CHUNKS[t][1]
+        for d, step in steps:
+            ship(
+                portion(t, (y + 3 * step) % Y), y_in[t].at[pl.ds(d * 2 * part, 2 * part)],
+                y_send.at[t], y_mid.at[t], (y + step) % Y,
+            )
+            ship(
+                portion(t, (y + 4) % Y).at[pl.ds(d * part, part)], y_in[t].at[pl.ds((4 + d) * part, part)],
+                y_send.at[t], y_mid.at[t], (y + 2 * step) % Y,
+            )
+        for d, step in steps:
+            ship(
+                portion(t, (y + step) % Y), y_in[t].at[pl.ds((6 + 2 * d) * part, 2 * part)],
+                y_send.at[t], y_recv.at[t], (y + step) % Y,
+            )
+
+    def second_round(t):
+        part = 4 * CHUNKS[t][1]
+        settle(y_in[t].at[pl.ds(0, 6 * part)], y_mid.at[t])
+        for d, step in steps:
+            to = (y + 2 * step) % Y
+            whole = portion(t, to)
+            whole[...] += y_in[t][d * 2 * part : (d + 1) * 2 * part, :]
+            whole[d * part : (d + 1) * part, :] += y_in[t][(4 + d) * part : (5 + d) * part, :]
+            ship(
+                whole, y_in[t].at[pl.ds((10 + 2 * d) * part, 2 * part)],
+                y_send.at[t], y_recv.at[t], to,
+            )
 
     my_pair = occ // 2
 
     def across_plane(t):
         r0, rows = CHUNKS[t]
-        settle(y_in[t].at[pl.ds(0, Y - 1)], y_recv.at[t])
-        settle(y_in[t].at[pl.ds(0, Y - 1)], y_send.at[t])
+        part = 4 * rows
+        settle(y_in[t].at[pl.ds(6 * part, 8 * part)], y_recv.at[t])
         total = grid[t][core, y // 2, half]
-        for k in range(1, Y):
-            total += y_in[t][(y + k) % Y]
+        for k in range(4):
+            total += y_in[t][(6 + 2 * k) * part : (8 + 2 * k) * part, :]
         y_out[t][...] = total.reshape(8, rows, LANES)
 
         def one(k, carry):
@@ -305,16 +349,15 @@
         def _():
             plane_in[t][zh * OWNERS + occ] = y_out[t][my_pair]
 
-    for t in range(n):
-        settle(recv_t[t].at[pl.ds(0, OWNERS - 1)], t_recv.at[t])
-        if t + 2 < n:
-            send_rows(t + 2)
-        ladder(t)
-        core_copy(t).start()
-        if t > 0:
-            across_plane(t - 1)
-        along_y(t)
-    across_plane(n - 1)
+    for t in range(n + 2):
+        if t < n:
+            ladder(t)
+        if 1 <= t <= n:
+            second_round(t - 1)
+        if t >= 2:
+            across_plane(t - 2)
+        if t < n:
+            first_round(t)
 
     group = (
         {"occ": occ, "sec": same_y + 1 - core},
@@ -359,21 +402,26 @@
 
     for t, (r0, rows) in enumerate(CHUNKS):
         settle(send_t.at[pl.ds(0, OWNERS - 1), pl.ds(r0, rows)], t_send.at[t])
+        settle(core_in[t], core_send.at[t])
+        settle(y_in[t], y_send.at[t])
 
 
 def shards(amplitudes, live_pairs, ladder_ints, cycle_ints, pair_ints, occ_energy, vir_energy):
     n = len(CHUNKS)
-    smem = pl.BlockSpec(memory_space=pltpu.SMEM)
     vmem = pl.BlockSpec(memory_space=pltpu.VMEM)
-    anywhere = pl.BlockSpec(memory_space=pl.ANY)
+    hbm = pl.BlockSpec(memory_space=pltpu.HBM)
     dma = pltpu.SemaphoreType.DMA
     rows = [r for _, r in CHUNKS]
     scratch = [
+        pltpu.SMEM((OWNERS,), jnp.int32),
+        pltpu.SMEM((OCCUPIED,), F32),
+        pltpu.SMEM((VIRTUAL,), F32),
+        pltpu.VMEM((COL_SHARE, OCCUPIED), F32),
         pltpu.VMEM((X, OCCUPIED * D_SHARE, LANES), F32),
         pltpu.VMEM((A_WINDOW, DEPTH, LANES), F32),
         pltpu.VMEM((OCCUPIED * D_SHARE, J_SHARE * LANES), F32),
-        pltpu.VMEM((DEPTH, A_WINDOW * LANES), BF16),
-        pltpu.VMEM((DEPTH, A_WINDOW * LANES), BF16),
+        pltpu.VMEM((3 * DEPTH, A_WINDOW * LANES), BF16),
+        pltpu.VMEM((OWNERS * max(rows), 3 * DEPTH), BF16),
         pltpu.VMEM((OCCUPIED * D_SHARE, J_SHARE * LANES), BF16),
         pltpu.VMEM((OCCUPIED * D_SHARE, J_SHARE * LANES), BF16),
         pltpu.VMEM((OWNERS, OCCUPIED, DEPTH), F32),
@@ -382,8 +430,9 @@
         pltpu.VMEM((J_SHARE, OWNERS * A_WINDOW, LANES), F32),
         pltpu.VMEM((OCCUPIED, LANES), F32),
         pltpu.VMEM((LANES, OCCUPIED), F32),
-        dma((3,)),
+        dma((7,)),
         dma((4,)),
+        dma((n,)),
         dma((n,)),
         dma((n,)),
         dma((n,)),
@@ -398,26 +447,31 @@
     scratch += [pltpu.VMEM((OWNERS, r, DEPTH), F32) for r in rows]
     scratch += [pltpu.VMEM((2, 4, 2, 8 * r, LANES), F32) for r in rows]
     scratch += [pltpu.VMEM((4, 2, 8 * r, LANES), F32) for r in rows]
-    scratch += [pltpu.VMEM((Y, 8 * r, LANES), F32) for r in rows]
+    scratch += [pltpu.VMEM((56 * r, LANES), F32) for r in rows]
     scratch += [pltpu.VMEM((8, r, LANES), F32) for r in rows]
     scratch += [pltpu.VMEM((32, r, LANES), F32) for r in rows]
     out = pl.pallas_call(
         kernel,
         out_shape=jax.ShapeDtypeStruct((COL_SHARE, OCCUPIED), F32),
-        in_specs=[smem, smem, smem, anywhere, anywhere, anywhere, vmem],
+        in_specs=[hbm] * 7,
         out_specs=vmem,
         scratch_shapes=scratch,
         compiler_params=pltpu.CompilerParams(
             collective_id=0, has_side_effects=True, vmem_limit_bytes=48 * 1024 * 1024
         ),
     )(
-        live_pairs,
-        occ_energy,
-        vir_energy,
-        amplitudes.transpose(0, 2, 1).reshape(OCCUPIED * D_SHARE, VIRTUAL),
-        ladder_ints.reshape(DEPTH, A_WINDOW * B_WINDOW),
-        cycle_ints.reshape(OCCUPIED * D_SHARE, J_SHARE * B_WINDOW),
-        pair_ints.T,
+        *(
+            pltpu.with_memory_space_constraint(array, pltpu.HBM)
+            for array in (
+                live_pairs,
+                occ_energy,
+                vir_energy,
+                amplitudes.transpose(0, 2, 1).reshape(OCCUPIED * D_SHARE, VIRTUAL),
+                ladder_ints.reshape(DEPTH, A_WINDOW * B_WINDOW),
+                cycle_ints.reshape(OCCUPIED * D_SHARE, J_SHARE * B_WINDOW),
+                pair_ints.T,
+            )
+        )
     )
     return out.T
 

time: 106 us -> 82.1 us (0.77)
  Pallas kernels: 97.5 us -> 81 us
  local copies, waits for them, and re-layouts: 7.58 us -> 0.61 us
    pallas_call x1, Pallas kernels: 97.5 us -> 81 us  [shards(): pl.pallas_call(kernel, out_shape=jax.ShapeDtypeStruct((COL_SHARE, OCCUPIE...]
    unnamed x15 -> x1, local copies, waits for them, and re-layouts: 7.58 us -> 0.61 us
where the time goes in v3:
time: 82.1 us; the launch traced here: 81.6 us
  Pallas kernels  81 us (99%)
    pallas_call x1, Pallas kernels, shards(): pl.pallas_call(kernel, out_shape=jax.ShapeDtypeStruct((COL_SHARE, OCCUPIE...  81 us

profile of v3, /device:TPU:1, one launch (start us, length us, event | category | flops | bytes accessed | tf_op | source)
XLA Modules:
  0.0 81.6 jit_solution(2569314528669530174)
XLA Ops:
  0.0 81.0 %shard_map.73 = f32[32,48]{1,0:T(8,128)S(1)} custom-call(s32[16]{0:T(128)} %live_hbm.1, f32[48]{0:T(128)} %occ_hbm.1, f32[512]{0:T(512)} %vir_hbm.1, f32[768,512]{1,0:T(8,128)} %bitcast.9, f32[512,1024]{1,0:T(8,128)} %bitcast.8, f32[768,384]{1,0:T(8,128)} %bitcast.10, f32[32,48]{1,0:T(8,128)} %bitcast.11), custom_call_target="tpu_custom_call" | custom-call | tf_op jit(solution)/shard_map/pallas_call | solution.py:453
  81.0 0.6 copy.9

commit v4 on v3

--- a/solution.py
+++ b/solution.py
@@ -21,6 +21,7 @@
 J_SHARE = OCCUPIED // OWNERS
 COL_SHARE = 32
 CHUNKS = tuple((8 * t, 8) for t in range(6))
+AHEAD = 3
 MESH = pl.DeviceIdType.MESH
 F32 = jnp.float32
 BF16 = jnp.bfloat16
@@ -45,12 +46,14 @@
 
 def kernel(
     live_hbm, occ_hbm, vir_hbm, t_hbm, w_hbm, u_hbm, pair_hbm, out_ref,
-    live_ref, occ_ref, vir_ref, pair_ref, t_v, w_v, u_v, w3, t3, uh, ul, send_t, cyc_own, cyc_all, cyc_out, final, turned,
-    local_sem, cyc_sem, t_send, t_recv, core_send, core_recv, y_send, y_mid, y_recv, p_send, p_recv,
+    live_ref, occ_ref, vir_ref, pair_ref, t_v, w_v, u_v, w3, t3, uh, ul, send_t, cyc_own, cyc_all, cyc_out, final, turned, bottom,
+    local_sem, cyc_sem, t_send, t_recv, core_send, core_recv, y_send, y_mid, y_recv, x_send, x_recv, p_send, p_recv,
     f_send, f_recv, *bufs,
 ):
     n = len(CHUNKS)
-    recv_t, grid, core_in, y_in, y_out, plane_in = (bufs[k * n : (k + 1) * n] for k in range(6))
+    recv_t, grid, core_in, y_in, y_out, x_in, x_out, plane_in = (
+        bufs[k * n : (k + 1) * n] for k in range(8)
+    )
     occ = lax.axis_index("occ")
     sec = lax.axis_index("sec")
     x, zl = occ // Z_LOW, occ % Z_LOW
@@ -61,10 +64,15 @@
 
     live_copy = pltpu.make_async_copy(live_hbm, live_ref, local_sem.at[3])
     live_copy.start()
-    for k in range(X):
-        pltpu.make_async_copy(
-            t_hbm.at[:, pl.ds(k * LANES, LANES)], t_v.at[k], local_sem.at[0]
-        ).start()
+    early = CHUNKS[0][1] * D_SHARE
+    late = OCCUPIED * D_SHARE - early
+    for part, (at, size) in enumerate(((0, early), (early, late))):
+        for k in range(X):
+            pltpu.make_async_copy(
+                t_hbm.at[pl.ds(at, size), pl.ds(k * LANES, LANES)],
+                t_v.at[k, pl.ds(at, size)],
+                local_sem.at[7 * part],
+            ).start()
     for k in range(A_WINDOW):
         pltpu.make_async_copy(
             w_hbm.at[:, pl.ds(k * LANES, LANES)], w_v.at[k], local_sem.at[1]
@@ -88,7 +96,7 @@
         return carry
 
     def greet_far(k, carry):
-        greet((occ + k) % OWNERS, (sec + 16) % 32)
+        greet(x * Z_LOW + k, (sec + 16) % 32)
         return carry
 
     def greet_y(k, carry):
@@ -96,7 +104,7 @@
         return carry
 
     lax.fori_loop(1, OWNERS, greet_occ, 0)
-    lax.fori_loop(0, OWNERS, greet_far, 0)
+    lax.fori_loop(0, Z_LOW, greet_far, 0)
     lax.fori_loop(1, Y, greet_y, 0)
     y_twin = y + 1 - 2 * half
     same_y = zh * 16 + y * 2
@@ -148,13 +156,15 @@
 
     live_copy.wait()
     live = live_ref[occ]
-    settle(t_v, local_sem.at[0])
+    settle(t_v.at[:, pl.ds(0, early)], local_sem.at[0])
+    relay(*CHUNKS[0])
+    pl.semaphore_wait(barrier, 28)
+    send_rows(0)
+    settle(t_v.at[:, pl.ds(early, late)], local_sem.at[7])
     for q in range(OCCUPIED * D_SHARE // LANES):
         rows = lax.broadcasted_iota(jnp.int32, (LANES, LANES), 0) // D_SHARE + q * (LANES // D_SHARE)
         block = jnp.where(rows < live, t_v[0, q * LANES : (q + 1) * LANES, :], 0.0)
         cyc_own[:, q * LANES : (q + 1) * LANES] = block.T[:A_WINDOW, :]
-    relay(*CHUNKS[0])
-    pl.semaphore_wait(barrier, 40)
 
     def cyc_z(k, carry):
         pltpu.make_async_remote_copy(
@@ -169,9 +179,9 @@
 
     lax.fori_loop(1, Z_LOW, cyc_z, 0)
     cyc_all[occ] = cyc_own[...]
-    send_rows(0)
-    relay(*CHUNKS[1])
-    send_rows(1)
+    for t in range(1, AHEAD):
+        relay(*CHUNKS[t])
+        send_rows(t)
 
     settle(cyc_all.at[pl.ds(0, Z_LOW - 1)], cyc_sem.at[1])
 
@@ -188,10 +198,6 @@
         return carry
 
     lax.fori_loop(1, X, cyc_x, 0)
-    for t in range(2, n):
-        relay(*CHUNKS[t])
-        send_rows(t)
-
     settle(w_v, local_sem.at[1])
 
     def weights(a, carry):
@@ -215,22 +221,23 @@
     for jj in range(J_SHARE):
         cyc_out[jj] = cyc[:, jj * LANES : (jj + 1) * LANES]
 
-    for copy in small:
-        copy.wait()
     wide = lax.broadcasted_iota(jnp.int32, (COL_SHARE, OCCUPIED), 1)
     tall = lax.broadcasted_iota(jnp.int32, (COL_SHARE, OCCUPIED), 0)
     sub = half * 2 + core
-    occ_pair = lax.fori_loop(
-        0, OCCUPIED, lambda j, v: jnp.where(wide == j, occ_ref[occ] + occ_ref[j], v),
-        jnp.zeros((COL_SHARE, OCCUPIED), F32),
-    )
-    vir_pair = lax.fori_loop(
-        0, COL_SHARE,
-        lambda b, v: jnp.where(tall == b, vir_ref[zh * 4 + y // 2] + vir_ref[sub * COL_SHARE + b], v),
-        jnp.zeros((COL_SHARE, OCCUPIED), F32),
-    )
-    bottom = occ_pair - vir_pair
-    alive = (wide < live).astype(F32)
+
+    def denominators():
+        for copy in small:
+            copy.wait()
+        occ_pair = lax.fori_loop(
+            0, OCCUPIED, lambda j, v: jnp.where(wide == j, occ_ref[occ] + occ_ref[j], v),
+            jnp.zeros((COL_SHARE, OCCUPIED), F32),
+        )
+        vir_pair = lax.fori_loop(
+            0, COL_SHARE,
+            lambda b, v: jnp.where(tall == b, vir_ref[zh * 4 + y // 2] + vir_ref[sub * COL_SHARE + b], v),
+            jnp.zeros((COL_SHARE, OCCUPIED), F32),
+        )
+        bottom[...] = occ_pair - vir_pair
 
     def core_piece(t, al):
         return pltpu.make_async_remote_copy(
@@ -245,16 +252,21 @@
     def ladder(t):
         settle(recv_t[t].at[pl.ds(0, OWNERS - 1)], t_recv.at[t])
         r0, rows = CHUNKS[t]
+        if t + AHEAD < n:
+            relay(*CHUNKS[t + AHEAD])
+            send_rows(t + AHEAD)
         high, low = halves(recv_t[t][...].reshape(OWNERS * rows, DEPTH))
         left = t3.at[pl.ds(0, OWNERS * rows)]
         left[:, :DEPTH] = high
         left[:, DEPTH : 2 * DEPTH] = low
         left[:, 2 * DEPTH :] = high
         for al in range(4):
-            cols = slice(al * 2 * LANES, (al + 1) * 2 * LANES)
-            out = 0.5 * jnp.dot(left[...], w3[:, cols], preferred_element_type=F32)
-            grid[t][0, al] = out[:, :LANES].reshape(2, 8 * rows, LANES)
-            grid[t][1, al] = out[:, LANES:].reshape(2, 8 * rows, LANES)
+            if al % 2 == 0:
+                cols = slice(al * 2 * LANES, (al + 2) * 2 * LANES)
+                out = 0.5 * jnp.dot(left[...], w3[:, cols], preferred_element_type=F32)
+                for q in range(4):
+                    piece = out[:, q * LANES : (q + 1) * LANES]
+                    grid[t][q % 2, al + q // 2] = piece.reshape(2, 8 * rows, LANES)
             for jj in range(J_SHARE):
                 row = occ * J_SHARE + jj - r0
 
@@ -315,9 +327,7 @@
                 y_send.at[t], y_recv.at[t], to,
             )
 
-    my_pair = occ // 2
-
-    def across_plane(t):
+    def along_x(t):
         r0, rows = CHUNKS[t]
         part = 4 * rows
         settle(y_in[t].at[pl.ds(6 * part, 8 * part)], y_recv.at[t])
@@ -326,38 +336,53 @@
             total += y_in[t][(6 + 2 * k) * part : (8 + 2 * k) * part, :]
         y_out[t][...] = total.reshape(8, rows, LANES)
 
-        def one(k, carry):
-            @pl.when(jnp.logical_not(jnp.logical_and(holder, k == my_pair)))
+        for k in range(1, X):
+            to = (x + k) % X
+            pltpu.make_async_remote_copy(
+                src_ref=y_out[t].at[pl.ds(2 * to, 2)],
+                dst_ref=x_in[t].at[k - 1],
+                send_sem=x_send.at[t],
+                recv_sem=x_recv.at[t],
+                device_id={"occ": to * Z_LOW + zl, "sec": sec},
+                device_id_type=MESH,
+            ).start()
+
+    def along_z(t):
+        settle(x_in[t], x_recv.at[t])
+        total = y_out[t][pl.ds(2 * x, 2)]
+        for k in range(X - 1):
+            total += x_in[t][k]
+        x_out[t][...] = total
+        for k in range(2):
+            mine = jnp.logical_and(holder, zl // 2 == k)
+
+            @pl.when(jnp.logical_not(mine))
             def _():
                 pltpu.make_async_remote_copy(
-                    src_ref=y_out[t].at[k],
-                    dst_ref=plane_in[t].at[zh * OWNERS + occ],
+                    src_ref=x_out[t].at[k],
+                    dst_ref=plane_in[t].at[zh * Z_LOW + zl],
                     send_sem=p_send.at[t],
                     recv_sem=p_recv.at[t],
-                    device_id={
-                        "occ": (k // 2) * Z_LOW + (k % 2) * 2 + half,
-                        "sec": core * 16 + y * 2 + core,
-                    },
+                    device_id={"occ": x * Z_LOW + 2 * k + half, "sec": core * 16 + y * 2 + core},
                     device_id_type=MESH,
                 ).start()
 
-            return carry
-
-        lax.fori_loop(0, 8, one, 0)
-
-        @pl.when(holder)
-        def _():
-            plane_in[t][zh * OWNERS + occ] = y_out[t][my_pair]
-
-    for t in range(n + 2):
+            @pl.when(mine)
+            def _():
+                plane_in[t][zh * Z_LOW + zl] = x_out[t][k]
+
+    for t in range(n + 4):
         if t < n:
             ladder(t)
-        if 1 <= t <= n:
+            first_round(t)
+        if 0 <= t - 4:
+            along_z(t - 4)
+        if 0 <= t - 3 < n:
+            along_x(t - 3)
+        if 0 <= t - 1 < n:
             second_round(t - 1)
-        if t >= 2:
-            across_plane(t - 2)
-        if t < n:
-            first_round(t)
+        if t == 0:
+            denominators()
 
     group = (
         {"occ": occ, "sec": same_y + 1 - core},
@@ -368,10 +393,10 @@
     @pl.when(holder)
     def _():
         for t, (r0, rows) in enumerate(CHUNKS):
-            settle(plane_in[t].at[pl.ds(0, 31)], p_recv.at[t])
-            settle(y_out[t].at[pl.ds(0, 7)], p_send.at[t])
+            settle(plane_in[t].at[pl.ds(0, 7)], p_recv.at[t])
+            settle(x_out[t].at[pl.ds(0, 1)], p_send.at[t])
             total = plane_in[t][0]
-            for k in range(1, 32):
+            for k in range(1, 8):
                 total += plane_in[t][k]
             final[r0 : r0 + rows, :] = total
         outs = [
@@ -393,17 +418,18 @@
     @pl.when(jnp.logical_not(holder))
     def _():
         for t in range(n):
-            settle(y_out[t], p_send.at[t])
+            settle(x_out[t], p_send.at[t])
         settle(final, f_recv)
 
     turned[...] = final[...].T
     summed = turned[pl.ds(pl.multiple_of(sub * COL_SHARE, COL_SHARE), COL_SHARE), :]
-    out_ref[...] = (summed + pair_ref[...]) / bottom * alive
+    out_ref[...] = (summed + pair_ref[...]) / bottom[...] * (wide < live).astype(F32)
 
     for t, (r0, rows) in enumerate(CHUNKS):
         settle(send_t.at[pl.ds(0, OWNERS - 1), pl.ds(r0, rows)], t_send.at[t])
         settle(core_in[t], core_send.at[t])
         settle(y_in[t], y_send.at[t])
+        settle(x_in[t], x_send.at[t])
 
 
 def shards(amplitudes, live_pairs, ladder_ints, cycle_ints, pair_ints, occ_energy, vir_energy):
@@ -430,8 +456,11 @@
         pltpu.VMEM((J_SHARE, OWNERS * A_WINDOW, LANES), F32),
         pltpu.VMEM((OCCUPIED, LANES), F32),
         pltpu.VMEM((LANES, OCCUPIED), F32),
-        dma((7,)),
+        pltpu.VMEM((COL_SHARE, OCCUPIED), F32),
+        dma((8,)),
         dma((4,)),
+        dma((n,)),
+        dma((n,)),
         dma((n,)),
         dma((n,)),
         dma((n,)),
@@ -449,7 +478,9 @@
     scratch += [pltpu.VMEM((4, 2, 8 * r, LANES), F32) for r in rows]
     scratch += [pltpu.VMEM((56 * r, LANES), F32) for r in rows]
     scratch += [pltpu.VMEM((8, r, LANES), F32) for r in rows]
-    scratch += [pltpu.VMEM((32, r, LANES), F32) for r in rows]
+    scratch += [pltpu.VMEM((X - 1, 2, r, LANES), F32) for r in rows]
+    scratch += [pltpu.VMEM((2, r, LANES), F32) for r in rows]
+    scratch += [pltpu.VMEM((8, r, LANES), F32) for r in rows]
     out = pl.pallas_call(
         kernel,
         out_shape=jax.ShapeDtypeStruct((COL_SHARE, OCCUPIED), F32),

time: 82.1 us -> 79 us (0.962)
  Pallas kernels: 81 us -> 77.9 us
    pallas_call x1, Pallas kernels: 81 us -> 77.9 us  [shards(): pl.pallas_call(kernel, out_shape=jax.ShapeDtypeStruct((COL_SHARE, OCCUPIE...]
where the time goes in v4:
time: 79 us; the launch traced here: 78.5 us
  Pallas kernels  77.9 us (99%)
    pallas_call x1, Pallas kernels, shards(): pl.pallas_call(kernel, out_shape=jax.ShapeDtypeStruct((COL_SHARE, OCCUPIE...  77.9 us

profile of v4, /device:TPU:1, one launch (start us, length us, event | category | flops | bytes accessed | tf_op | source)
XLA Modules:
  0.0 78.5 jit_solution(17594798604089780195)
XLA Ops:
  0.0 77.9 %shard_map.73 = f32[32,48]{1,0:T(8,128)S(1)} custom-call(s32[16]{0:T(128)} %live_hbm.1, f32[48]{0:T(128)} %occ_hbm.1, f32[512]{0:T(512)} %vir_hbm.1, f32[768,512]{1,0:T(8,128)} %bitcast.9, f32[512,1024]{1,0:T(8,128)} %bitcast.8, f32[768,384]{1,0:T(8,128)} %bitcast.10, f32[32,48]{1,0:T(8,128)} %bitcast.11), custom_call_target="tpu_custom_call" | custom-call | tf_op jit(solution)/shard_map/pallas_call | solution.py:484
  77.9 0.6 copy.9

commit v5 on v4

--- a/solution.py
+++ b/solution.py
@@ -66,13 +66,43 @@
     live_copy.start()
     early = CHUNKS[0][1] * D_SHARE
     late = OCCUPIED * D_SHARE - early
-    for part, (at, size) in enumerate(((0, early), (early, late))):
+    def fetch_rows(part, at, size):
         for k in range(X):
             pltpu.make_async_copy(
                 t_hbm.at[pl.ds(at, size), pl.ds(k * LANES, LANES)],
                 t_v.at[k, pl.ds(at, size)],
                 local_sem.at[7 * part],
             ).start()
+
+    fetch_rows(0, 0, early)
+
+    barrier = pltpu.get_barrier_semaphore()
+
+    def greet(o, s):
+        pl.semaphore_signal(barrier, inc=1, device_id={"occ": o, "sec": s}, device_id_type=MESH)
+
+    def greet_occ(k, carry):
+        greet((occ + k) % OWNERS, sec)
+        return carry
+
+    def greet_far(k, carry):
+        greet(x * Z_LOW + k, (sec + 16) % 32)
+        return carry
+
+    def greet_y(k, carry):
+        greet(occ, zh * 16 + ((y + k) % Y) * 2 + core)
+        return carry
+
+    lax.fori_loop(1, OWNERS, greet_occ, 0)
+    lax.fori_loop(0, Z_LOW, greet_far, 0)
+    lax.fori_loop(1, Y, greet_y, 0)
+    y_twin = y + 1 - 2 * half
+    same_y = zh * 16 + y * 2
+    twin_y = zh * 16 + y_twin * 2
+    greet(occ, same_y + 1 - core)
+    greet(occ, twin_y + 1 - core)
+
+    fetch_rows(1, early, late)
     for k in range(A_WINDOW):
         pltpu.make_async_copy(
             w_hbm.at[:, pl.ds(k * LANES, LANES)], w_v.at[k], local_sem.at[1]
@@ -85,32 +115,6 @@
     )
     for copy in small:
         copy.start()
-
-    barrier = pltpu.get_barrier_semaphore()
-
-    def greet(o, s):
-        pl.semaphore_signal(barrier, inc=1, device_id={"occ": o, "sec": s}, device_id_type=MESH)
-
-    def greet_occ(k, carry):
-        greet((occ + k) % OWNERS, sec)
-        return carry
-
-    def greet_far(k, carry):
-        greet(x * Z_LOW + k, (sec + 16) % 32)
-        return carry
-
-    def greet_y(k, carry):
-        greet(occ, zh * 16 + ((y + k) % Y) * 2 + core)
-        return carry
-
-    lax.fori_loop(1, OWNERS, greet_occ, 0)
-    lax.fori_loop(0, Z_LOW, greet_far, 0)
-    lax.fori_loop(1, Y, greet_y, 0)
-    y_twin = y + 1 - 2 * half
-    same_y = zh * 16 + y * 2
-    twin_y = zh * 16 + y_twin * 2
-    greet(occ, same_y + 1 - core)
-    greet(occ, twin_y + 1 - core)
 
     lane_group = lax.broadcasted_iota(jnp.int32, (8, LANES), 1) // C_SHARE
     sub_row = lax.broadcasted_iota(jnp.int32, (8, LANES), 0)
@@ -371,10 +375,34 @@
             def _():
                 plane_in[t][zh * Z_LOW + zl] = x_out[t][k]
 
+    group = (
+        {"occ": occ, "sec": same_y + 1 - core},
+        {"occ": occ, "sec": twin_y + core},
+        {"occ": occ, "sec": twin_y + 1 - core},
+    )
+
+    def share(t):
+        @pl.when(holder)
+        def _():
+            r0, rows = CHUNKS[t]
+            settle(plane_in[t].at[pl.ds(0, 7)], p_recv.at[t])
+            total = plane_in[t][0]
+            for k in range(1, 8):
+                total += plane_in[t][k]
+            final[r0 : r0 + rows, :] = total
+            for k, to in enumerate(group):
+                piece = final.at[pl.ds(r0, rows)]
+                pltpu.make_async_remote_copy(
+                    src_ref=piece, dst_ref=piece, send_sem=f_send.at[k], recv_sem=f_recv,
+                    device_id=to, device_id_type=MESH,
+                ).start()
+
     for t in range(n + 4):
         if t < n:
             ladder(t)
             first_round(t)
+        if 0 <= t - 5:
+            share(t - 5)
         if 0 <= t - 4:
             along_z(t - 4)
         if 0 <= t - 3 < n:
@@ -383,42 +411,10 @@
             second_round(t - 1)
         if t == 0:
             denominators()
-
-    group = (
-        {"occ": occ, "sec": same_y + 1 - core},
-        {"occ": occ, "sec": twin_y + core},
-        {"occ": occ, "sec": twin_y + 1 - core},
-    )
-
-    @pl.when(holder)
-    def _():
-        for t, (r0, rows) in enumerate(CHUNKS):
-            settle(plane_in[t].at[pl.ds(0, 7)], p_recv.at[t])
-            settle(x_out[t].at[pl.ds(0, 1)], p_send.at[t])
-            total = plane_in[t][0]
-            for k in range(1, 8):
-                total += plane_in[t][k]
-            final[r0 : r0 + rows, :] = total
-        outs = [
-            pltpu.make_async_remote_copy(
-                src_ref=final,
-                dst_ref=final,
-                send_sem=f_send.at[k],
-                recv_sem=f_recv,
-                device_id=to,
-                device_id_type=MESH,
-            )
-            for k, to in enumerate(group)
-        ]
-        for copy in outs:
-            copy.start()
-        for copy in outs:
-            copy.wait_send()
+    share(n - 1)
 
     @pl.when(jnp.logical_not(holder))
     def _():
-        for t in range(n):
-            settle(x_out[t], p_send.at[t])
         settle(final, f_recv)
 
     turned[...] = final[...].T
@@ -430,6 +426,18 @@
         settle(core_in[t], core_send.at[t])
         settle(y_in[t], y_send.at[t])
         settle(x_in[t], x_send.at[t])
+        @pl.when(holder)
+        def _():
+            settle(x_out[t].at[pl.ds(0, 1)], p_send.at[t])
+
+        @pl.when(jnp.logical_not(holder))
+        def _():
+            settle(x_out[t], p_send.at[t])
+
+    @pl.when(holder)
+    def _():
+        for k in range(3):
+            settle(final, f_send.at[k])
 
 
 def shards(amplitudes, live_pairs, ladder_ints, cycle_ints, pair_ints, occ_energy, vir_energy):

time: 79 us -> 78.8 us (level)
  no operation moved by 1% of the time
where the time goes in v5:
time: 78.8 us; the launch traced here: 78.5 us
  Pallas kernels  77.9 us (99%)
    pallas_call x1, Pallas kernels, shards(): pl.pallas_call(kernel, out_shape=jax.ShapeDtypeStruct((COL_SHARE, OCCUPIE...  77.9 us

profile of v5, /device:TPU:1, one launch (start us, length us, event | category | flops | bytes accessed | tf_op | source)
XLA Modules:
  0.0 78.5 jit_solution(13278018254905066267)
XLA Ops:
  0.0 77.9 %shard_map.73 = f32[32,48]{1,0:T(8,128)S(1)} custom-call(s32[16]{0:T(128)} %live_hbm.1, f32[48]{0:T(128)} %occ_hbm.1, f32[512]{0:T(512)} %vir_hbm.1, f32[768,512]{1,0:T(8,128)} %bitcast.9, f32[512,1024]{1,0:T(8,128)} %bitcast.8, f32[768,384]{1,0:T(8,128)} %bitcast.10, f32[32,48]{1,0:T(8,128)} %bitcast.11), custom_call_target="tpu_custom_call" | custom-call | tf_op jit(solution)/shard_map/pallas_call | solution.py:492
  77.9 0.6 copy.9
